TPU v7x, 32 devices: a whole 2x2x4 slice. The times are simulated.
32 devices in a mesh: groups: 1, expert: 8 (over z, core), dp: 4 (over y, x).
Axes of the slice: x: 2, y: 2, z: 4, core: 2. Of those that a mesh axis runs over, the one named last changes fastest.
Arguments:
- tokens: bfloat16 [128, 4096], P(('groups', 'expert', 'dp')), may hold values from -6 to 6
- expert_ids: int32 [128, 2], P(('groups', 'expert', 'dp')), may hold values from 0 to 7, as said below
- gate_weights: bfloat16 [128, 2], P(('groups', 'expert', 'dp')), may hold values from 0.099609375 to 1
- placement: int32 [2, 2], P('groups'), may hold values from 0 to 7, as said below
- w_gate: bfloat16 [8, 1536, 4096], P('expert', 'dp'), may hold values from -0.09375 to 0.09375
- w_up: bfloat16 [8, 1536, 4096], P('expert', 'dp'), may hold values from -0.09375 to 0.09375
- w_down: bfloat16 [8, 1536, 4096], P('expert', 'dp'), may hold values from -0.15625 to 0.15625
Outputs:
- mixed: bfloat16 [128, 4096], P(('groups', 'expert', 'dp'))
Inputs may be any that keep to these rules, and one draw needn't show every extreme that they name: `expert_ids`: each row names 2 different experts. In each aligned block of 16 rows (the tokens of one index of expert) no expert is named by more than 6 rows, and some expert is named by exactly that many. `placement`: row 0 holds 2 different experts; row 1 holds 2 different expert indices, none of which appears in row 0.
All inputs are finite; a program needn't handle non-finite values.
Results may differ from a plain program's by a relative error of at most 0.015.
Values may be sent and summed in bfloat16 or wider, within the bound.
A program may use at most 64 MiB of HBM per device.

v0:
```python
import jax
import jax.numpy as jnp
from jax import lax
from jax.sharding import PartitionSpec as P


def expert_block(rows, gate_w, up_w, down_w):
    contract = (((1,), (1,)), ((), ()))
    gate = lax.dot_general(rows, gate_w, contract, preferred_element_type=jnp.float32)
    up = lax.dot_general(rows, up_w, contract, preferred_element_type=jnp.float32)
    hidden = (jax.nn.silu(gate) * up).astype(jnp.bfloat16)
    return jnp.dot(hidden, down_w, preferred_element_type=jnp.float32).astype(jnp.bfloat16)


def body(tokens, expert_ids, gate_weights, placement, w_gate, w_up, w_down):
    group_source, group_gates = (
        lax.all_gather(tokens, "dp", axis=0, tiled=True),
        lax.all_gather(gate_weights, "dp", axis=0, tiled=True),
    )
    group_ids = lax.all_gather(expert_ids, "dp", axis=0, tiled=True)
    experts = lax.axis_size("expert")
    my_index = lax.axis_index("expert")
    width = tokens.shape[1]
    group = group_ids.shape[0]
    topk = expert_ids.shape[1]
    first = max(2, group * topk // experts)
    second = max(1, first // 2)
    slots = first + second
    pair_ids = group_ids.reshape(-1)
    onehot = (pair_ids[:, None] == jnp.arange(experts, dtype=jnp.int32)[None, :]).astype(jnp.int32)
    rank = jnp.sum((jnp.cumsum(onehot, axis=0) - onehot) * onehot, axis=1)
    match = pair_ids[:, None] == placement[0][None, :]
    listed = jnp.any(match, axis=1)
    keep = (rank < first) | listed & (rank < slots)
    dest = jnp.where(keep, pair_ids * slots + rank, -1)
    row_iota = jnp.arange(experts * slots, dtype=jnp.int32)
    pick = (dest[None, :] == row_iota[:, None]).reshape(experts * slots, group, topk)
    select = jnp.any(pick, axis=2).astype(jnp.bfloat16)
    weights_rows = jnp.sum(
        jnp.where(pick, group_gates[None, :, :].astype(jnp.float32), 0.0), axis=2
    ).astype(jnp.bfloat16)
    send = jnp.dot(select, group_source, preferred_element_type=jnp.float32).astype(jnp.bfloat16)
    received = lax.all_to_all(
        send.reshape(experts, slots, width), "expert", split_axis=0, concat_axis=0, tiled=True
    )
    main = expert_block(received[:, :first].reshape(-1, width), w_gate[0], w_up[0], w_down[0])
    active = jnp.any(placement[0] == my_index)
    extra_weights = (w_gate[0], w_up[0], w_down[0])
    extra_rows = received[:, first:].reshape(-1, width)
    extra = lax.cond(
        active,
        lambda: expert_block(extra_rows, extra_weights[0], extra_weights[1], extra_weights[2]),
        lambda: jnp.zeros((experts * second, width), jnp.bfloat16),
    )
    partial_value = jnp.concatenate(
        [main.reshape(experts, first, width), extra.reshape(experts, second, width)], axis=1
    )
    contract = (((0,), (0,)), ((), ()))
    summed = lax.psum_scatter(
        partial_value.astype(jnp.float32).astype(jnp.bfloat16),
        "dp",
        scatter_dimension=2,
        tiled=True,
    ).astype(jnp.float32)
    back = lax.all_to_all(
        summed.astype(jnp.bfloat16), "expert", split_axis=0, concat_axis=0, tiled=True
    ).astype(summed.dtype)
    group_cols = lax.dot_general(
        weights_rows.astype(jnp.float32),
        back.reshape(experts * slots, -1),
        contract,
        precision=lax.Precision.HIGHEST,
        preferred_element_type=jnp.float32,
    )
    mine_out = lax.all_to_all(
        group_cols.astype(jnp.bfloat16), "dp", split_axis=0, concat_axis=1, tiled=True
    ).astype(group_cols.dtype)
    return mine_out.astype(jnp.bfloat16)


def solution(mesh):
    placed = (
        P(("groups", "expert", "dp"), None),
        P(("groups", "expert", "dp"), None),
        P(("groups", "expert", "dp"), None),
        P("groups", None),
        P("expert", "dp", None),
        P("expert", "dp", None),
        P("expert", "dp", None),
    )
    return jax.shard_map(
        body,
        mesh=mesh,
        in_specs=placed,
        out_specs=P(("groups", "expert", "dp"), None),
        check_vma=False,
    )
```

profile of v0, /device:TPU:0, one launch (start us, length us, event | category | flops | bytes accessed | tf_op | source)
XLA Modules:
  0.0 121.7 jit_solution(14547632915415462673)
XLA Ops:
  6.5 9.9 %all-gather = s32[4,4,2]{1,2,0:T(2,128)S(1)} all-gather(s32[1,4,2]{1,2,0:T(2,128)} %bitcast.40), channel_id=1, replica_groups=mesh['groups'=1,'expert'=8,'dp'=4] {'dp'}, dimensions={0}, use_global_device_ids=true | all-gather | bytes 160 | tf_op jit(solution)/shard_map/all_gather | solution.py:20
  16.9 0.2 select_reduce_fusion.1
  17.2 0.7 slice_bitcast_fusion
  18.3 8.3 %all-gather.2 = bf16[4,4,4096]{2,1,0:T(4,128)(2,1)S(1)} all-gather(bf16[1,4,4096]{2,1,0:T(4,128)(2,1)} %bitcast.38), channel_id=1, replica_groups=mesh['groups'=1,'expert'=8,'dp'=4] {'dp'}, dimensions={0}, use_global_device_ids=true | all-gather | bytes 163840 | tf_op jit(solution)/shard_map/all_gather | solution.py:17
  26.6 0.7 reshape.64
  27.2 1.2 convolution_convert_fusion.1
  28.5 0.9 reshape.55
  29.4 4.9 %all-to-all-start = ((bf16[8,6,4096]{2,1,0:T(8,128)(2,1)}), bf16[8,6,4096]{2,1,0:T(8,128)(2,1)}, u32[]{:S(2)}, u32[]{:S(2)}) async-start(bf16[8,6,4096]{2,1,0:T(8,128)(2,1)} %reshape.55), calls=%async_computation | async-start | bytes 1048576 | tf_op jit(solution)/shard_map/all_to_all | solution.py:43
  34.3 1.3 %compare_reduce_fusion = pred[]{:T(512)} fusion(s32[]{:T(128)S(6)} %axis_index.15, s32[2,2]{1,0:T(2,128)} %param.12), kind=kLoop, calls=%fused_computation.32 | loop fusion | flops 3 | bytes 13 | tf_op jit(solution)/shard_map/reduce_or | solution.py:47
  36.3 13.4 %all-to-all-done = bf16[8,6,4096]{2,1,0:T(8,128)(2,1)} async-done(((bf16[8,6,4096]{2,1,0:T(8,128)(2,1)}), bf16[8,6,4096]{2,1,0:T(8,128)(2,1)}, u32[]{:S(2)}, u32[]{:S(2)}) %all-to-all-start) | async-done | bytes 393248 | tf_op jit(solution)/shard_map/all_to_all | solution.py:43
  49.7 1.8 %slice.13 = bf16[8,4,4096]{2,1,0:T(4,128)(2,1)} slice(bf16[8,6,4096]{2,1,0:T(8,128)(2,1)} %all-to-all-done), slice={[0:8], [0:4], [0:4096]} | slice | bytes 524288 | tf_op jit(solution)/shard_map/slice | solution.py:46
  51.5 1.0 reshape.56
  52.6 1.0 fusion.21
  53.6 5.6 %convolution_convert_fusion.2 = bf16[32,4096]{1,0:T(8,128)(2,1)} fusion(bf16[32,4096]{1,0:T(8,128)(2,1)S(1)} %reshape.56, f32[32,384]{1,0:T(8,128)S(1)} %fusion.21, bf16[1,384,4096]{2,1,0:T(8,128)(2,1)} %param.15, bf16[1,384,4096]{2,1,0:T(8,128)(2,1)} %param.14), kind=kOutput, calls=%fused_computation.11 | convolution fusion | flops 201531392 | bytes 6864896 | tf_op jit(solution)/shard_map/dot_general | solution.py:12
  59.2 1.1 reshape.57
  60.3 0.7 conditional.1
  60.3 0.7 reshape.48
  61.0 1.9 %pad_maximum_fusion = bf16[8,6,4096]{2,1,0:T(8,128)(2,1)} fusion(bf16[8,2,4096]{2,1,0:T(2,128)(2,1)} %get-tuple-element.23, bf16[8,4,4096]{2,1,0:T(4,128)(2,1)S(1)} %reshape.57), kind=kLoop, calls=%fused_computation.15 | loop fusion | flops 786432 | bytes 786432 | tf_op jit(solution)/shard_map/concatenate | solution.py:55
  63.0 7.2 %all-gather.1 = bf16[4,4,2]{1,2,0:T(2,128)(2,1)S(1)} all-gather(bf16[1,4,2]{1,2,0:T(2,128)(2,1)S(1)} %bitcast.41), channel_id=1, replica_groups=mesh['groups'=1,'expert'=8,'dp'=4] {'dp'}, dimensions={0}, use_global_device_ids=true | all-gather | bytes 80 | tf_op jit(solution)/shard_map/all_gather | solution.py:18
  70.2 25.2 %reduce-scatter.2.cloned.1.call-done = bf16[8,6,1024]{2,1,0:T(8,128)(2,1)} async-done(((bf16[8,6,4096]{2,1,0:T(8,128)(2,1)}), bf16[8,6,1024]{2,1,0:T(8,128)(2,1)}) %reduce-scatter.2.cloned.1.call-update) | async-done | bytes 98320 | tf_op jit(solution)/shard_map/reduce_scatter | solution.py:59
  95.4 4.6 %all-to-all-start.1 = ((bf16[8,6,1024]{2,1,0:T(8,128)(2,1)}), bf16[8,6,1024]{2,1,0:T(8,128)(2,1)S(1)}, u32[]{:S(2)}, u32[]{:S(2)}) async-start(bf16[8,6,1024]{2,1,0:T(8,128)(2,1)} %reduce-scatter.2.cloned.1.call-done), calls=%async_computation.2 | async-start | bytes 262144 | tf_op jit(solution)/shard_map/all_to_all | solution.py:65
  100.2 6.6 %all-to-all-done.1 = bf16[8,6,1024]{2,1,0:T(8,128)(2,1)S(1)} async-done(((bf16[8,6,1024]{2,1,0:T(8,128)(2,1)}), bf16[8,6,1024]{2,1,0:T(8,128)(2,1)S(1)}, u32[]{:S(2)}, u32[]{:S(2)}) %all-to-all-start.1) | async-done | bytes 98336 | tf_op jit(solution)/shard_map/all_to_all | solution.py:65
  106.9 7.3 %all_to_all.29 = bf16[4,4,1024]{2,1,0:T(4,128)(2,1)S(1)} all-to-all(bf16[4,4,1024]{2,1,0:T(4,128)(2,1)S(1)} %all_to_all.22), channel_id=1, replica_groups=mesh['groups'=1,'expert'=8,'dp'=4] {'dp'}, dimensions={0} | all-to-all | bytes 65536 | tf_op jit(solution)/shard_map/all_to_all | solution.py:75
  114.2 0.6 copy.44
  (24 shorter events, 1.3 us)
Async XLA Ops:
  6.5 46.0 %copy-start = (bf16[1,384,4096]{2,1,0:T(8,128)(2,1)S(1)}, bf16[1,384,4096]{2,1,0:T(8,128)(2,1)}, u32[]{:S(2)}) copy-start(bf16[1,384,4096]{2,1,0:T(8,128)(2,1)} %param.13) | copy-start | bytes 9437188
  29.4 20.3 %all-to-all-start = ((bf16[8,6,4096]{2,1,0:T(8,128)(2,1)}), bf16[8,6,4096]{2,1,0:T(8,128)(2,1)}, u32[]{:S(2)}, u32[]{:S(2)}) async-start(bf16[8,6,4096]{2,1,0:T(8,128)(2,1)} %reshape.55), calls=%async_computation | async-start | bytes 1048576 | tf_op jit(solution)/shard_map/all_to_all | solution.py:43
  34.3 61.1 %reduce-scatter.2.cloned.1.call-start = ((), (), s32[]{:S(2)}) async-start(), calls=%async_computation.4 | async-start | bytes 655360 | tf_op jit(solution)/shard_map/reduce_scatter | solution.py:59
  60.2 2.7 %copy-start.1 = (bf16[4,2]{0,1:T(2,128)(2,1)S(1)}, bf16[4,2]{0,1:T(2,128)(2,1)}, u32[]{:S(2)}) copy-start(bf16[4,2]{0,1:T(2,128)(2,1)} %param.11) | copy-start | bytes 52
  95.4 11.4 %all-to-all-start.1 = ((bf16[8,6,1024]{2,1,0:T(8,128)(2,1)}), bf16[8,6,1024]{2,1,0:T(8,128)(2,1)S(1)}, u32[]{:S(2)}, u32[]{:S(2)}) async-start(bf16[8,6,1024]{2,1,0:T(8,128)(2,1)} %reduce-scatter.2.cloned.1.call-done), calls=%async_computation.2 | async-start | bytes 262144 | tf_op jit(solution)/shard_map/all_to_all | solution.py:65
Sparse Core Ops, SparseCore 0:
  63.1 32.2 reduce-scatter.1
where the time goes:
time: 122 us
  waiting for transfers between devices  45.2 us (37%)
  blocking collectives  32.7 us (27%)
  between operations  14.1 us (12%)
  starting transfers between devices  9.54 us (8%)
  local copies, waits for them, and re-layouts  8.28 us (7%)
  matrix products  7.95 us (7%)
  other arithmetic  3.84 us (3%)
    reduce_scatter x1, waiting for transfers between devices, body(): lax.psum_scatter(partial_value.astype(jnp.float32).astype(jnp.bfloat16),...  25.2 us
    all_to_all x1, waiting for transfers between devices, body(): lax.all_to_all(send.reshape(experts, slots, width), 'expert', split_axis=...  13.4 us
    all_gather x1, blocking collectives, body(): group_ids = lax.all_gather(expert_ids, 'dp', axis=0, tiled=True)  9.95 us
    all_gather x1, blocking collectives, body(): lax.all_gather(tokens, 'dp', axis=0, tiled=True)  8.3 us
    all_to_all x1, blocking collectives, body(): lax.all_to_all(group_cols.astype(jnp.bfloat16), 'dp', split_axis=0, conca...  7.29 us
    all_gather x1, blocking collectives, body(): lax.all_gather(gate_weights, 'dp', axis=0, tiled=True)  7.17 us
    all_to_all x1, waiting for transfers between devices, body(): lax.all_to_all(summed.astype(jnp.bfloat16), 'expert', split_axis=0, conca...  6.58 us
    dot_general x1, matrix products, expert_block(): jnp.dot(hidden, down_w, preferred_element_type=jnp.float32)  5.59 us
  transfers between devices with their start and end apart: 3, of which 3 were waited for; matrix products, arithmetic and copies ran while one was open for 1% of the time, Pallas kernels for 0%

commit v1 on v0

--- a/solution.py
+++ b/solution.py
@@ -2,6 +2,37 @@
 import jax.numpy as jnp
 from jax import lax
 from jax.sharding import PartitionSpec as P
+
+
+def _pair_scales(x_in, ndim_at, values):
+    opened = x_in.shape
+    prior = x_in.reshape(
+        *opened[:ndim_at], values, opened[ndim_at] // values, *opened[ndim_at + 1 :]
+    )
+    return jnp.moveaxis(prior, ndim_at, 0)
+
+
+def perform_quotas(w_in, pos_dim):
+    all_values = list(w_in.shape[1:])
+    all_values[pos_dim] *= w_in.shape[0]
+    return jnp.moveaxis(w_in, 0, pos_dim).reshape(all_values)
+
+
+def positions_tell(x_part, ax_name, panel, q_in):
+    local_now = lax.axis_size(ax_name)
+    next_value, v1 = (local_now, lax.axis_index(ax_name))
+    plain = _pair_scales(x_part, panel, next_value)
+    line_up = [plain[v1]]
+    for tick in range(1, next_value):
+        raw_out = plain[(v1 + tick) % next_value]
+        aux = lax.ppermute(
+            raw_out,
+            axis_name=ax_name,
+            perm=[(it, (it + tick) % next_value) for it in range(next_value)],
+        )
+        line_up.append(aux)
+    plain = jnp.stack(line_up)[(v1 - jnp.arange(next_value)) % next_value]
+    return perform_quotas(plain, q_in)
 
 
 def expert_block(rows, gate_w, up_w, down_w):
@@ -72,9 +103,7 @@
         precision=lax.Precision.HIGHEST,
         preferred_element_type=jnp.float32,
     )
-    mine_out = lax.all_to_all(
-        group_cols.astype(jnp.bfloat16), "dp", split_axis=0, concat_axis=1, tiled=True
-    ).astype(group_cols.dtype)
+    mine_out = positions_tell(group_cols.astype(jnp.bfloat16), "dp", 0, 1).astype(group_cols.dtype)
     return mine_out.astype(jnp.bfloat16)
 
 

time: 122 us -> 123 us (level)
  blocking collectives: 32.7 us -> 25.4 us
  waiting for transfers between devices: 45.2 us -> 49.2 us
  starting transfers between devices: 9.54 us -> 13.1 us
    all_to_all x1 -> x0, blocking collectives: 7.29 us -> none  [body(): lax.all_to_all(group_cols.astype(jnp.bfloat16), 'dp', split_axis=0, conca...]
    ppermute x0 -> x3, waiting for transfers between devices: none -> 3.98 us  [positions_tell(): lax.ppermute(raw_out, axis_name=ax_name, perm=[(it, (it + tick) % next_va...]
    ppermute x0 -> x3, starting transfers between devices: none -> 3.54 us  [positions_tell(): lax.ppermute(raw_out, axis_name=ax_name, perm=[(it, (it + tick) % next_va...]
  transfers between devices with their start and end apart: 3 -> 6, of which waited for: 3 -> 6; matrix products, arithmetic and copies ran while one was open for 1% -> 1% of each run, Pallas kernels for 0% -> 0%
where the time goes in v1:
time: 123 us
  waiting for transfers between devices  49.2 us (40%)
  blocking collectives  25.4 us (21%)
  between operations  14.2 us (12%)
  starting transfers between devices  13.1 us (11%)
  local copies, waits for them, and re-layouts  8.88 us (7%)
  matrix products  7.95 us (6%)
  other arithmetic  3.89 us (3%)
    reduce_scatter x1, waiting for transfers between devices, body(): lax.psum_scatter(partial_value.astype(jnp.float32).astype(jnp.bfloat16),...  25.1 us
    all_to_all x1, waiting for transfers between devices, body(): lax.all_to_all(send.reshape(experts, slots, width), 'expert', split_axis=...  13.4 us
    all_gather x1, blocking collectives, body(): group_ids = lax.all_gather(expert_ids, 'dp', axis=0, tiled=True)  9.95 us
    all_gather x1, blocking collectives, body(): lax.all_gather(tokens, 'dp', axis=0, tiled=True)  8.3 us
    all_gather x1, blocking collectives, body(): lax.all_gather(gate_weights, 'dp', axis=0, tiled=True)  7.17 us
    all_to_all x1, waiting for transfers between devices, body(): lax.all_to_all(summed.astype(jnp.bfloat16), 'expert', split_axis=0, conca...  6.66 us
    dot_general x1, matrix products, expert_block(): jnp.dot(hidden, down_w, preferred_element_type=jnp.float32)  5.59 us
    all_to_all x1, starting transfers between devices, body(): lax.all_to_all(send.reshape(experts, slots, width), 'expert', split_axis=...  4.88 us
  transfers between devices with their start and end apart: 6, of which 6 were waited for; matrix products, arithmetic and copies ran while one was open for 1% of the time, Pallas kernels for 0%

profile of v1, /device:TPU:0, one launch (start us, length us, event | category | flops | bytes accessed | tf_op | source)
XLA Modules:
  0.0 122.6 jit_solution(4002861759043062737)
XLA Ops:
  6.5 9.9 %all-gather = s32[4,4,2]{1,2,0:T(2,128)S(1)} all-gather(s32[1,4,2]{1,2,0:T(2,128)} %bitcast.53), channel_id=1, replica_groups=mesh['groups'=1,'expert'=8,'dp'=4] {'dp'}, dimensions={0}, use_global_device_ids=true | all-gather | bytes 160 | tf_op jit(solution)/shard_map/all_gather | solution.py:51
  18.3 8.3 %all-gather.2 = bf16[4,4,4096]{2,1,0:T(4,128)(2,1)S(1)} all-gather(bf16[1,4,4096]{2,1,0:T(4,128)(2,1)} %bitcast.48), channel_id=1, replica_groups=mesh['groups'=1,'expert'=8,'dp'=4] {'dp'}, dimensions={0}, use_global_device_ids=true | all-gather | bytes 163840 | tf_op jit(solution)/shard_map/all_gather | solution.py:48
  27.2 1.2 convolution_convert_fusion.1
  28.5 0.9 reshape.107
  29.4 4.9 %all-to-all-start = ((bf16[8,6,4096]{2,1,0:T(8,128)(2,1)}), bf16[8,6,4096]{2,1,0:T(8,128)(2,1)}, u32[]{:S(2)}, u32[]{:S(2)}) async-start(bf16[8,6,4096]{2,1,0:T(8,128)(2,1)} %reshape.107), calls=%async_computation | async-start | bytes 1048576 | tf_op jit(solution)/shard_map/all_to_all | solution.py:74
  34.3 1.3 %compare_reduce_fusion = pred[]{:T(512)} fusion(s32[]{:T(128)S(6)} %axis_index.23, s32[2,2]{1,0:T(2,128)} %param.12), kind=kLoop, calls=%fused_computation.42 | loop fusion | flops 3 | bytes 13 | tf_op jit(solution)/shard_map/reduce_or | solution.py:78
  36.3 13.4 %all-to-all-done = bf16[8,6,4096]{2,1,0:T(8,128)(2,1)} async-done(((bf16[8,6,4096]{2,1,0:T(8,128)(2,1)}), bf16[8,6,4096]{2,1,0:T(8,128)(2,1)}, u32[]{:S(2)}, u32[]{:S(2)}) %all-to-all-start) | async-done | bytes 393248 | tf_op jit(solution)/shard_map/all_to_all | solution.py:74
  49.7 1.8 %slice.15 = bf16[8,4,4096]{2,1,0:T(4,128)(2,1)} slice(bf16[8,6,4096]{2,1,0:T(8,128)(2,1)} %all-to-all-done), slice={[0:8], [0:4], [0:4096]} | slice | bytes 524288 | tf_op jit(solution)/shard_map/slice | solution.py:77
  51.5 1.0 reshape.108
  52.6 1.0 fusion.23
  53.6 5.6 %convolution_convert_fusion.2 = bf16[32,4096]{1,0:T(8,128)(2,1)} fusion(bf16[32,4096]{1,0:T(8,128)(2,1)S(1)} %reshape.108, f32[32,384]{1,0:T(8,128)S(1)} %fusion.23, bf16[1,384,4096]{2,1,0:T(8,128)(2,1)} %param.15, bf16[1,384,4096]{2,1,0:T(8,128)(2,1)} %param.14), kind=kOutput, calls=%fused_computation.12 | convolution fusion | flops 201531392 | bytes 6864896 | tf_op jit(solution)/shard_map/dot_general | solution.py:43
  59.2 1.1 reshape.109
  60.3 0.7 conditional.1
  60.3 0.7 reshape.98
  61.0 1.9 %pad_maximum_fusion = bf16[8,6,4096]{2,1,0:T(8,128)(2,1)} fusion(bf16[8,2,4096]{2,1,0:T(2,128)(2,1)} %get-tuple-element.27, bf16[8,4,4096]{2,1,0:T(4,128)(2,1)S(1)} %reshape.109), kind=kLoop, calls=%fused_computation.16 | loop fusion | flops 786432 | bytes 786432 | tf_op jit(solution)/shard_map/concatenate | solution.py:86
  63.0 7.2 %all-gather.1 = bf16[4,4,2]{1,2,0:T(2,128)(2,1)S(1)} all-gather(bf16[1,4,2]{1,2,0:T(2,128)(2,1)S(1)} %bitcast.54), channel_id=1, replica_groups=mesh['groups'=1,'expert'=8,'dp'=4] {'dp'}, dimensions={0}, use_global_device_ids=true | all-gather | bytes 80 | tf_op jit(solution)/shard_map/all_gather | solution.py:49
  70.2 25.1 %reduce-scatter.2.cloned.1.call-done = bf16[8,6,1024]{2,1,0:T(8,128)(2,1)} async-done(((bf16[8,6,4096]{2,1,0:T(8,128)(2,1)}), bf16[8,6,1024]{2,1,0:T(8,128)(2,1)}) %reduce-scatter.2.cloned.1.call-update) | async-done | bytes 98320 | tf_op jit(solution)/shard_map/reduce_scatter | solution.py:90
  95.4 4.6 %all-to-all-start.1 = ((bf16[8,6,1024]{2,1,0:T(8,128)(2,1)}), bf16[8,6,1024]{2,1,0:T(8,128)(2,1)S(1)}, u32[]{:S(2)}, u32[]{:S(2)}) async-start(bf16[8,6,1024]{2,1,0:T(8,128)(2,1)} %reduce-scatter.2.cloned.1.call-done), calls=%async_computation.2 | async-start | bytes 262144 | tf_op jit(solution)/shard_map/all_to_all | solution.py:96
  100.1 6.7 %all-to-all-done.1 = bf16[8,6,1024]{2,1,0:T(8,128)(2,1)S(1)} async-done(((bf16[8,6,1024]{2,1,0:T(8,128)(2,1)}), bf16[8,6,1024]{2,1,0:T(8,128)(2,1)S(1)}, u32[]{:S(2)}, u32[]{:S(2)}) %all-to-all-start.1) | async-done | bytes 98336 | tf_op jit(solution)/shard_map/all_to_all | solution.py:96
  107.0 1.5 %collective-permute-start.2 = (bf16[4,1024]{1,0:T(4,128)(2,1)S(1)}, bf16[4,1024]{1,0:T(4,128)(2,1)S(1)}, u32[]{:S(2)}, u32[]{:S(2)}) collective-permute-start(bf16[4,1024]{1,0:T(4,128)(2,1)S(1)} %get-tuple-element.24), channel_id=1, source_target_pairs={{0,3},{1,0},{2,1},{3,2},{4,7},{5,4},{6,5},{7,6},{8,11},{9,8},{10,9... | collective-permute-start | bytes 24584 | tf_op jit(solution)/shard_map/ppermute | solution.py:28
  108.5 1.5 %collective-permute-start.1 = (bf16[4,1024]{1,0:T(4,128)(2,1)S(1)}, bf16[4,1024]{1,0:T(4,128)(2,1)S(1)}, u32[]{:S(2)}, u32[]{:S(2)}) collective-permute-start(bf16[4,1024]{1,0:T(4,128)(2,1)S(1)} %get-tuple-element.25), channel_id=1, source_target_pairs={{0,2},{1,3},{2,0},{3,1},{4,6},{5,7},{6,4},{7,5},{8,10},{9,11},{10,... | collective-permute-start | bytes 24584 | tf_op jit(solution)/shard_map/ppermute | solution.py:28
  110.7 1.5 %collective-permute-done.1 = bf16[4,1024]{1,0:T(4,128)(2,1)S(1)} collective-permute-done((bf16[4,1024]{1,0:T(4,128)(2,1)S(1)}, bf16[4,1024]{1,0:T(4,128)(2,1)S(1)}, u32[]{:S(2)}, u32[]{:S(2)}) %collective-permute-start.1) | collective-permute-done | bytes 8224 | tf_op jit(solution)/shard_map/ppermute | solution.py:28
  112.1 2.4 %collective-permute-done = bf16[4,1024]{1,0:T(4,128)(2,1)S(1)} collective-permute-done((bf16[4,1024]{1,0:T(4,128)(2,1)S(1)}, bf16[4,1024]{1,0:T(4,128)(2,1)S(1)}, u32[]{:S(2)}, u32[]{:S(2)}) %collective-permute-start) | collective-permute-done | bytes 8224 | tf_op jit(solution)/shard_map/ppermute | solution.py:28
  114.5 1.2 gather_fusion
  (33 shorter events, 3.6 us)
Async XLA Ops:
  6.5 46.0 %copy-start = (bf16[1,384,4096]{2,1,0:T(8,128)(2,1)S(1)}, bf16[1,384,4096]{2,1,0:T(8,128)(2,1)}, u32[]{:S(2)}) copy-start(bf16[1,384,4096]{2,1,0:T(8,128)(2,1)} %param.13) | copy-start | bytes 9437188
  29.4 20.3 %all-to-all-start = ((bf16[8,6,4096]{2,1,0:T(8,128)(2,1)}), bf16[8,6,4096]{2,1,0:T(8,128)(2,1)}, u32[]{:S(2)}, u32[]{:S(2)}) async-start(bf16[8,6,4096]{2,1,0:T(8,128)(2,1)} %reshape.107), calls=%async_computation | async-start | bytes 1048576 | tf_op jit(solution)/shard_map/all_to_all | solution.py:74
  34.3 61.1 %reduce-scatter.2.cloned.1.call-start = ((), (), s32[]{:S(2)}) async-start(), calls=%async_computation.3 | async-start | bytes 655360 | tf_op jit(solution)/shard_map/reduce_scatter | solution.py:90
  60.2 2.7 %copy-start.1 = (bf16[4,2]{0,1:T(2,128)(2,1)S(1)}, bf16[4,2]{0,1:T(2,128)(2,1)}, u32[]{:S(2)}) copy-start(bf16[4,2]{0,1:T(2,128)(2,1)} %param.11) | copy-start | bytes 52
  95.4 11.4 %all-to-all-start.1 = ((bf16[8,6,1024]{2,1,0:T(8,128)(2,1)}), bf16[8,6,1024]{2,1,0:T(8,128)(2,1)S(1)}, u32[]{:S(2)}, u32[]{:S(2)}) async-start(bf16[8,6,1024]{2,1,0:T(8,128)(2,1)} %reduce-scatter.2.cloned.1.call-done), calls=%async_computation.2 | async-start | bytes 262144 | tf_op jit(solution)/shard_map/all_to_all | solution.py:96
  107.0 3.7 %collective-permute-start.2 = (bf16[4,1024]{1,0:T(4,128)(2,1)S(1)}, bf16[4,1024]{1,0:T(4,128)(2,1)S(1)}, u32[]{:S(2)}, u32[]{:S(2)}) collective-permute-start(bf16[4,1024]{1,0:T(4,128)(2,1)S(1)} %get-tuple-element.24), channel_id=1, source_target_pairs={{0,3},{1,0},{2,1},{3,2},{4,7},{5,4},{6,5},{7,6},{8,11},{9,8},{10,9... | collective-permute-start | bytes 24584 | tf_op jit(solution)/shard_map/ppermute | solution.py:28
  108.5 3.7 %collective-permute-start.1 = (bf16[4,1024]{1,0:T(4,128)(2,1)S(1)}, bf16[4,1024]{1,0:T(4,128)(2,1)S(1)}, u32[]{:S(2)}, u32[]{:S(2)}) collective-permute-start(bf16[4,1024]{1,0:T(4,128)(2,1)S(1)} %get-tuple-element.25), channel_id=1, source_target_pairs={{0,2},{1,3},{2,0},{3,1},{4,6},{5,7},{6,4},{7,5},{8,10},{9,11},{10,... | collective-permute-start | bytes 24584 | tf_op jit(solution)/shard_map/ppermute | solution.py:28
  110.0 4.5 %collective-permute-start = (bf16[4,1024]{1,0:T(4,128)(2,1)S(1)}, bf16[4,1024]{1,0:T(4,128)(2,1)S(1)}, u32[]{:S(2)}, u32[]{:S(2)}) collective-permute-start(bf16[4,1024]{1,0:T(4,128)(2,1)S(1)} %get-tuple-element.26), channel_id=1, source_target_pairs={{0,1},{1,2},{2,3},{3,0},{4,5},{5,6},{6,7},{7,4},{8,9},{9,10},{10,1... | collective-permute-start | bytes 24584 | tf_op jit(solution)/shard_map/ppermute | solution.py:28
Sparse Core Ops, SparseCore 0:
  63.1 32.2 reduce-scatter.1
